TPU v7x, 32 devices: a whole 2x2x4 slice. The times are simulated.
32 devices in a mesh: group: 2 (over y), tile: 4 (over x, core), seq: 4 (over z).
Axes of the slice: x: 2, y: 2, z: 4, core: 2. Of those that a mesh axis runs over, the one named last changes fastest.
Arguments:
- hidden: bfloat16 [8, 1024, 3072], P(('group', 'tile'), 'seq'), parts along dimension 0
- modulation: float32 [10, 3072], P('group'), parts along dimension 0, may hold values from -3 to 3
- w_qkv: bfloat16 [3072, 9216], P('tile', 'seq')
- w_out: bfloat16 [3072, 3072], P('seq', 'tile'), may hold values from -0.109375 to 0.109375
- w_head: bfloat16 [3072, 64], replicated, may hold values from -0.109375 to 0.109375
- latent: float32 [8, 1024, 64], P(('group', 'tile'), 'seq'), parts along dimension 0, may hold values from -6 to 6
- weights_int: int32 [8, 1024], P(('group', 'tile'), 'seq'), parts along dimension 0, may hold values from 1 to 8
- step_index: int32 [2], P('group'), parts along dimension 0, may hold values from 0 to 13
Outputs:
- stepped: float32 [8, 1024, 64], P(('group', 'tile'), 'seq'), parts along dimension 0
- clean: float32 [8, 1024, 64], P(('group', 'tile'), 'seq'), parts along dimension 0
There are 2 independent parts, one for each index of `group`. A program takes and returns all parts, laid end to end along the dimension named above; an argument that names none is the same for every part. Nothing has to cross between parts.
All inputs are finite; a program needn't handle non-finite values.
Results may differ from a plain program's by a relative error of at most 0.0055.
Values may be sent and summed in bfloat16 or wider, within the bound.
A program may use at most 64 MiB of HBM per device.

v0:
```python
import math
import jax
import jax.numpy as jnp
from jax import lax
from jax.sharding import PartitionSpec as P

HD = 128
NSTEPS = 28


def shifted(value, axis, steps):
    count = lax.axis_size(axis)
    leading, last = (max(0, -steps), min(count, count - steps))
    return lax.ppermute(value, axis, [(source, source + steps) for source in range(leading, last)])


def layer_norm(values):
    mean = jnp.mean(values, axis=-1, keepdims=True)
    centred = values - mean
    spread = jnp.mean(centred * centred, axis=-1, keepdims=True)
    return centred * lax.rsqrt(spread + 1e-06)


def root_norm(values):
    return values * lax.rsqrt(jnp.mean(values * values, axis=-1, keepdims=True) + 1e-06)


def noise_level(index, steps):
    level = 1.0 - index / steps
    return 3.0 * level / (1.0 + 2.0 * level)


def shards(hidden, modulation, w_qkv, w_out, w_head, latent, weights_int, step_index):
    local = hidden[0].astype(jnp.float32)
    norm_in = (layer_norm(local) * (1.0 + modulation[1]) + modulation[0]).astype(jnp.bfloat16)
    gathered = lax.all_gather(norm_in, "seq", axis=0, tiled=True)
    length = gathered.shape[0]
    heads_here = w_qkv.shape[1] // (3 * HD)
    projected = jnp.dot(
        gathered,
        lax.all_gather(w_qkv, "tile", axis=0, tiled=True),
        preferred_element_type=jnp.float32,
    )
    full_out = lax.all_gather(w_out, "tile", axis=1, tiled=True)
    projected = projected.reshape(length, heads_here, 3, HD)
    queries = root_norm(projected[:, :, 0]).astype(jnp.bfloat16)
    keys = root_norm(projected[:, :, 1]).astype(jnp.bfloat16)
    values = projected[:, :, 2].astype(jnp.bfloat16)
    block = min(512, length)
    scale = 1.0 / math.sqrt(HD)
    pieces = []
    for first in range(0, length, block):
        scores = (
            jnp.einsum(
                "qhe,khe->hqk",
                queries[first : first + block],
                keys,
                preferred_element_type=jnp.float32,
            )
            * scale
        )
        expo = jnp.exp(scores)
        probs = (expo / jnp.sum(expo, axis=-1, keepdims=True)).astype(jnp.bfloat16)
        pieces.append(
            jnp.einsum("hqk,khe->qhe", probs, values, preferred_element_type=jnp.float32).astype(
                jnp.bfloat16
            )
        )
    attended = jnp.concatenate(pieces, axis=0).reshape(length, heads_here * HD)
    summed = lax.psum_scatter(
        jnp.dot(attended, full_out, preferred_element_type=jnp.float32).astype(jnp.bfloat16),
        "seq",
        scatter_dimension=0,
        tiled=True,
    ).astype(jnp.float32)
    mixed = local + modulation[2] * summed
    norm_out = (layer_norm(mixed) * (1.0 + modulation[4]) + modulation[3]).astype(jnp.bfloat16)
    velocity = jnp.dot(norm_out, w_head, preferred_element_type=jnp.float32)
    index = step_index[0].astype(jnp.float32)
    now = noise_level(index, NSTEPS)
    after = noise_level(index + 1.0, NSTEPS)
    base = latent[0]
    weight = weights_int[0].astype(jnp.float32)
    moved = base + (after - now) * velocity
    guess = base - now * velocity
    weighted = jnp.concatenate([moved, guess], axis=1) * weight[:, None]
    seq_count = lax.axis_size("seq")
    place = lax.axis_index("seq")
    prev_tile = (
        shifted(weighted.astype(jnp.bfloat16), "tile", 1).astype(weighted.dtype),
        shifted(weight.astype(jnp.bfloat16), "tile", 1).astype(weight.dtype),
    )
    prev_sums, prev_weight = (
        shifted(prev_tile[0].astype(jnp.bfloat16), "seq", -(seq_count - 2)).astype(jnp.float32),
        shifted(prev_tile[1].astype(jnp.bfloat16), "seq", -(seq_count - 2)).astype(jnp.float32),
    )
    next_tile = (
        shifted(weighted.astype(jnp.bfloat16), "tile", -1).astype(weighted.dtype),
        shifted(weight.astype(jnp.bfloat16), "tile", -1).astype(weight.dtype),
    )
    next_sums, next_weight = (
        shifted(next_tile[0].astype(jnp.bfloat16), "seq", seq_count - 2).astype(jnp.float32),
        shifted(next_tile[1].astype(jnp.bfloat16), "seq", seq_count - 2).astype(jnp.float32),
    )
    take_prev = place < 2
    take_next = place >= seq_count - 2
    totals = weighted + jnp.where(take_prev, prev_sums, 0.0) + jnp.where(take_next, next_sums, 0.0)
    norms = weight + jnp.where(take_prev, prev_weight, 0.0) + jnp.where(take_next, next_weight, 0.0)
    joined = totals / norms[:, None]
    channels = velocity.shape[1]
    return (joined[None, :, :channels], joined[None, :, channels:])


def solution(mesh):
    in_specs = (
        P(("group", "tile"), "seq", None),
        P("group", None),
        P("tile", "seq"),
        P("seq", "tile"),
        P(),
        P(("group", "tile"), "seq", None),
        P(("group", "tile"), "seq"),
        P("group"),
    )
    out_specs = (P(("group", "tile"), "seq", None), P(("group", "tile"), "seq", None))
    return jax.shard_map(shards, mesh=mesh, in_specs=in_specs, out_specs=out_specs, check_vma=False)
```

profile of v0, /device:TPU:26, one launch (start us, length us, event | category | flops | bytes accessed | tf_op | source)
XLA Modules:
  0.0 437.2 jit_solution(16859526870282650366)
XLA Ops:
  7.2 1.9 fusion.30
  9.1 1.7 convert_reduce_fusion
  10.8 2.0 fusion.8
  12.8 1.9 fusion.11
  14.8 0.7 all-gather.6.cloned.1.call-update
  16.3 112.1 %all-gather.4.cloned.1.call-done = bf16[1024,3072]{1,0:T(8,128)(2,1)} async-done(((bf16[256,3072]{1,0:T(8,128)(2,1)}), bf16[1024,3072]{1,0:T(8,128)(2,1)}) %all-gather.4.cloned.1.call-update) | async-done | bytes 6291472 | tf_op jit(solution)/shard_map/all_gather | solution.py:36
  128.4 92.7 %all-gather.6.cloned.1.call-done = bf16[3072,2304]{1,0:T(8,128)(2,1)} async-done(((bf16[768,2304]{1,0:T(8,128)(2,1)}), bf16[3072,2304]{1,0:T(8,128)(2,1)}) %all-gather.6.cloned.1.call-update) | async-done | bytes 14155792 | tf_op jit(solution)/shard_map/all_gather | solution.py:41
  221.1 19.6 %fusion.31 = f32[1024,2304]{0,1:T(8,128)S(1)} fusion(bf16[1024,3072]{1,0:T(8,128)(2,1)} %all-gather.4.cloned.1.call-done, bf16[3072,2304]{1,0:T(8,128)(2,1)} %all-gather.6.cloned.1.call-done), kind=kOutput, calls=%fused_computation.60 | convolution fusion | flops 14495514624 | bytes 29884416 | tf_op jit(solution)/shard_map/dot_general | solution.py:39
  240.7 3.5 copy-done.3
  244.2 2.0 slice.50
  246.3 3.6 copy.21
  249.9 2.9 fusion.12
  252.8 2.3 multiply_reduce_fusion.1
  255.2 1.0 fusion.13
  256.2 8.2 %fusion = (f32[6,512]{1,0:T(8,128)S(1)}, f32[6,512,1024]{2,1,0:T(8,128)}) fusion(f32[1024,6,3,128]{0,3,2,1:T(8,128)} %bitcast.78, f32[1024,6]{0,1:T(8,128)S(1)} %add_rsqrt_fusion, bf16[1024,6,128]{2,0,1:T(8,128)(2,1)S(1)} %fusion.13), kind=kOutput, calls=%fused_computation.4 | convolution fusion | flops 813167616 | bytes 16560128 | tf_op jit(solution)/shard_map/qhe,khe->hqk/dot_general | solution.py:54
  264.5 2.7 fusion.1
  267.1 6.0 %fusion.19 = bf16[512,6,128]{0,2,1:T(8,128)(2,1)S(1)} fusion(f32[6,512,1024]{2,1,0:T(8,128)} %get-tuple-element.14, f32[6,512]{1,0:T(8,128)S(1)} %get-tuple-element.13, f32[1024,6,3,128]{0,3,2,1:T(8,128)S(1)} %bitcast.82), kind=kOutput, calls=%fused_computation.35 | convolution fusion | flops 815136768 | bytes 14958592 | tf_op jit(solution)/shard_map/hqk,khe->qhe/dot_general | solution.py:65
  273.1 2.9 fusion.20
  276.3 9.5 %convolution_convert_fusion = bf16[1024,3072]{1,0:T(8,128)(2,1)} fusion(bf16[1024,768]{0,1:T(8,128)(2,1)S(1)} %bitcast.84, bf16[768,3072]{1,0:T(8,128)(2,1)} %all-gather.8.cloned.1.call-done), kind=kOutput, calls=%fused_computation.8 | convolution fusion | flops 4834983936 | bytes 12582912 | tf_op jit(solution)/shard_map/dot_general | solution.py:71
  286.6 110.6 %reduce-scatter.2.cloned.1.call-done = bf16[256,3072]{1,0:T(8,128)(2,1)} async-done(((bf16[1024,3072]{1,0:T(8,128)(2,1)}), bf16[256,3072]{1,0:T(8,128)(2,1)}) %reduce-scatter.2.cloned.1.call-update) | async-done | bytes 1572880 | tf_op jit(solution)/shard_map/reduce_scatter | solution.py:70
  397.2 2.1 fusion.14
  399.4 0.8 multiply_reduce_fusion
  400.2 1.1 bitcast_add_fusion
  401.3 1.9 collective-permute-start
  403.3 3.6 collective-permute-start.2
  406.9 1.9 collective-permute-start.4
  408.9 3.6 collective-permute-start.6
  412.5 2.9 collective-permute-start.5
  415.5 1.3 collective-permute-start.7
  416.8 5.4 %collective-permute-start.1 = (bf16[256,128]{0,1:T(8,128)(2,1)S(1)}, bf16[256,128]{0,1:T(8,128)(2,1)S(1)}, u32[]{:S(2)}, u32[]{:S(2)}) collective-permute-start(bf16[256,128]{0,1:T(8,128)(2,1)S(1)} %collective-permute-done), channel_id=1, source_target_pairs={{2,0},{3,1},{6,4},{7,5},{10,8},{11,9},{14,12},{15,13},{18,16},{19,... | collective-permute-start | bytes 196616 | tf_op jit(solution)/shard_map/ppermute | solution.py:14
  422.2 1.3 collective-permute-start.3
  424.1 5.9 %collective-permute-done.3 = bf16[256,128]{0,1:T(8,128)(2,1)S(1)} collective-permute-done((bf16[256,128]{0,1:T(8,128)(2,1)S(1)}, bf16[256,128]{0,1:T(8,128)(2,1)S(1)}, u32[]{:S(2)}, u32[]{:S(2)}) %collective-permute-start.3) | collective-permute-done | bytes 65568 | tf_op jit(solution)/shard_map/ppermute | solution.py:14
  (52 shorter events, 2.5 us)
Async XLA Ops:
  7.2 393.0 %copy-start = (bf16[3072,64]{0,1:T(8,128)(2,1)S(1)}, bf16[3072,64]{0,1:T(8,128)(2,1)}, u32[]{:S(2)}) copy-start(bf16[3072,64]{0,1:T(8,128)(2,1)} %param.12) | copy-start | bytes 1179652
  7.2 5.6 %copy-start.1 = (bf16[1,256,3072]{2,1,0:T(8,128)(2,1)S(1)}, bf16[1,256,3072]{2,1,0:T(8,128)(2,1)}, u32[]{:S(2)}) copy-start(bf16[1,256,3072]{2,1,0:T(8,128)(2,1)} %param.8) | copy-start | bytes 4718596
  7.2 121.2 %all-gather.4.cloned.1.call-start = ((), (), s32[]{:S(2)}) async-start(), calls=%async_computation.1 | async-start | bytes 7864320 | tf_op jit(solution)/shard_map/all_gather | solution.py:36
  14.8 206.3 %all-gather.6.cloned.1.call-start = ((), (), s32[]{:S(2)}) async-start(), calls=%async_computation.2 | async-start | bytes 17694720 | tf_op jit(solution)/shard_map/all_gather | solution.py:41
  15.5 260.8 %all-gather.8.cloned.1.call-start = ((), (), s32[]{:S(2)}) async-start(), calls=%async_computation.3 | async-start | bytes 5898240 | tf_op jit(solution)/shard_map/all_gather | solution.py:44
  16.3 381.0 %reduce-scatter.2.cloned.1.call-start = ((), (), s32[]{:S(2)}) async-start(), calls=%async_computation.4 | async-start | bytes 7864320 | tf_op jit(solution)/shard_map/reduce_scatter | solution.py:70
  240.7 3.6 copy-start.3
  249.9 5.3 %copy-start.2 = (f32[1024,6,1,128]{3,0,1,2:T(8,128)S(1)}, f32[1024,6,1,128]{3,0,1,2:T(8,128)}, u32[]{:S(2)}) copy-start(f32[1024,6,1,128]{3,0,1,2:T(8,128)} %copy.21) | copy-start | bytes 9437188
  255.2 9.2 %slice-start = ((s8[9437184]{0:T(1024)(128)(4,1)}), s8[4194304]{0:T(1024)(128)(4,1)S(1)}, s32[]{:S(2)}) async-start(s8[9437184]{0:T(1024)(128)(4,1)} %bitcast.79), calls=%async_computation.5 | async-start | bytes 8388608
  256.2 8.3 %slice-start.1 = ((s8[9437184]{0:T(1024)(128)(4,1)}), s8[4194304]{0:T(1024)(128)(4,1)S(1)}, s32[]{:S(2)}) async-start(s8[9437184]{0:T(1024)(128)(4,1)} %bitcast.79), calls=%async_computation.6 | async-start | bytes 8388608
  256.2 8.2 %slice-start.2 = ((s8[9437184]{0:T(1024)(128)(4,1)}), s8[1048576]{0:T(1024)(128)(4,1)S(1)}, s32[]{:S(2)}) async-start(s8[9437184]{0:T(1024)(128)(4,1)} %bitcast.79), calls=%async_computation.7 | async-start | bytes 2097152
  285.8 0.7 copy-start.7
  397.2 2.1 copy-start.4
  397.2 3.0 copy-start.5
  397.2 3.0 copy-start.6
  397.2 3.0 copy-start.8
  401.3 15.4 %collective-permute-start = (bf16[256,128]{0,1:T(8,128)(2,1)S(1)}, bf16[256,128]{0,1:T(8,128)(2,1)S(1)}, u32[]{:S(2)}, u32[]{:S(2)}) collective-permute-start(bf16[256,128]{0,1:T(8,128)(2,1)S(1)} %fusion.27), channel_id=1, source_target_pairs={{0,4},{4,8},{8,12},{1,5},{5,9},{9,13},{2,6},{6,10},{10,14},{3,7},{... | collective-permute-start | bytes 196616 | tf_op jit(solution)/shard_map/ppermute | solution.py:14
  403.3 19.0 %collective-permute-start.2 = (bf16[256,128]{0,1:T(8,128)(2,1)S(1)}, bf16[256,128]{0,1:T(8,128)(2,1)S(1)}, u32[]{:S(2)}, u32[]{:S(2)}) collective-permute-start(bf16[256,128]{0,1:T(8,128)(2,1)S(1)} %fusion.27), channel_id=1, source_target_pairs={{4,0},{8,4},{12,8},{5,1},{9,5},{13,9},{6,2},{10,6},{14,10},{7,3},{... | collective-permute-start | bytes 196616 | tf_op jit(solution)/shard_map/ppermute | solution.py:14
  406.9 5.6 %collective-permute-start.4 = (bf16[256]{0:T(256)(128)(2,1)S(1)}, bf16[256]{0:T(256)(128)(2,1)S(1)}, u32[]{:S(2)}, u32[]{:S(2)}) collective-permute-start(bf16[256]{0:T(256)(128)(2,1)S(1)} %convert_element_type.109), channel_id=1, source_target_pairs={{0,4},{4,8},{8,12},{1,5},{5,9},{9,13},{2,6},{6,10},{10,14},{3,7},{... | collective-permute-start | bytes 1544 | tf_op jit(solution)/shard_map/ppermute | solution.py:14
  408.9 6.6 %collective-permute-start.6 = (bf16[256]{0:T(256)(128)(2,1)S(1)}, bf16[256]{0:T(256)(128)(2,1)S(1)}, u32[]{:S(2)}, u32[]{:S(2)}) collective-permute-start(bf16[256]{0:T(256)(128)(2,1)S(1)} %convert_element_type.109), channel_id=1, source_target_pairs={{4,0},{8,4},{12,8},{5,1},{9,5},{13,9},{6,2},{10,6},{14,10},{7,3},{... | collective-permute-start | bytes 1544 | tf_op jit(solution)/shard_map/ppermute | solution.py:14
  412.5 11.0 %collective-permute-start.5 = (bf16[256]{0:T(256)(128)(2,1)S(1)}, bf16[256]{0:T(256)(128)(2,1)S(1)}, u32[]{:S(2)}, u32[]{:S(2)}) collective-permute-start(bf16[256]{0:T(256)(128)(2,1)S(1)} %collective-permute-done.4), channel_id=1, source_target_pairs={{2,0},{3,1},{6,4},{7,5},{10,8},{11,9},{14,12},{15,13},{18,16},{19,... | collective-permute-start | bytes 1544 | tf_op jit(solution)/shard_map/ppermute | solution.py:14
  415.5 8.1 %collective-permute-start.7 = (bf16[256]{0:T(256)(128)(2,1)S(1)}, bf16[256]{0:T(256)(128)(2,1)S(1)}, u32[]{:S(2)}, u32[]{:S(2)}) collective-permute-start(bf16[256]{0:T(256)(128)(2,1)S(1)} %collective-permute-done.6), channel_id=1, source_target_pairs={{0,2},{1,3},{4,6},{5,7},{8,10},{9,11},{12,14},{13,15},{16,18},{17,... | collective-permute-start | bytes 1544 | tf_op jit(solution)/shard_map/ppermute | solution.py:14
  416.8 7.3 %collective-permute-start.1 = (bf16[256,128]{0,1:T(8,128)(2,1)S(1)}, bf16[256,128]{0,1:T(8,128)(2,1)S(1)}, u32[]{:S(2)}, u32[]{:S(2)}) collective-permute-start(bf16[256,128]{0,1:T(8,128)(2,1)S(1)} %collective-permute-done), channel_id=1, source_target_pairs={{2,0},{3,1},{6,4},{7,5},{10,8},{11,9},{14,12},{15,13},{18,16},{19,... | collective-permute-start | bytes 196616 | tf_op jit(solution)/shard_map/ppermute | solution.py:14
  422.2 7.7 %collective-permute-start.3 = (bf16[256,128]{0,1:T(8,128)(2,1)S(1)}, bf16[256,128]{0,1:T(8,128)(2,1)S(1)}, u32[]{:S(2)}, u32[]{:S(2)}) collective-permute-start(bf16[256,128]{0,1:T(8,128)(2,1)S(1)} %collective-permute-done.2), channel_id=1, source_target_pairs={{0,2},{1,3},{4,6},{5,7},{8,10},{9,11},{12,14},{13,15},{16,18},{17,... | collective-permute-start | bytes 196616 | tf_op jit(solution)/shard_map/ppermute | solution.py:14
Sparse Core Ops, SparseCore 0:
  14.9 113.4 all-gather.3
  129.9 91.1 all-gather.5
  222.6 37.4 all-gather.7
  286.0 111.1 reduce-scatter.1
where the time goes:
time: 438 us; the launch traced here: 437 us
  waiting for transfers between devices  323 us (74%)
  matrix products  50 us (11%)
  starting transfers between devices  22.2 us (5%)
  other arithmetic  17 us (4%)
  between operations  14.9 us (3%)
  local copies, waits for them, and re-layouts  9.9 us (2%)
    all_gather x1, waiting for transfers between devices, shards(): gathered = lax.all_gather(norm_in, 'seq', axis=0, tiled=True)  112 us
    reduce_scatter x1, waiting for transfers between devices, shards(): lax.psum_scatter(jnp.dot(attended, full_out, preferred_element_type=jnp.f...  111 us
    all_gather x1, waiting for transfers between devices, shards(): lax.all_gather(w_qkv, 'tile', axis=0, tiled=True)  92.7 us
    ppermute x8, starting transfers between devices, shifted(): lax.ppermute(value, axis, [(source, source + steps) for source in range(l...  22.1 us
    dot_general x1, matrix products, shards(): jnp.dot(gathered, lax.all_gather(w_qkv, 'tile', axis=0, tiled=True), pref...  19.6 us
    dot_general x2, matrix products, shards(): jnp.einsum('qhe,khe->hqk', queries[first:first + block], keys, preferred_...  10.9 us
    dot_general x1, matrix products, shards(): jnp.dot(attended, full_out, preferred_element_type=jnp.float32)  9.54 us
    dot_general x2, matrix products, shards(): jnp.einsum('hqk,khe->qhe', probs, values, preferred_element_type=jnp.floa...  8.92 us
  transfers between devices with their start and end apart: 12, of which 5 were waited for; matrix products, arithmetic and copies ran while one was open for 12% of the time, Pallas kernels for 0%

commit v1 on v0

--- a/solution.py
+++ b/solution.py
@@ -6,6 +6,17 @@
 
 HD = 128
 NSTEPS = 28
+
+
+def ring_gather(x, axis, dim):
+    ways = lax.axis_size(axis)
+    pieces = [x]
+    for far in range(1, ways):
+        pieces.append(
+            lax.ppermute(pieces[far - 1], axis, [(d, (d - 1) % ways) for d in range(ways)])
+        )
+    line = jnp.concatenate(pieces, axis=dim)
+    return jnp.roll(line, lax.axis_index(axis) * x.shape[dim], axis=dim)
 
 
 def shifted(value, axis, steps):
@@ -36,11 +47,7 @@
     gathered = lax.all_gather(norm_in, "seq", axis=0, tiled=True)
     length = gathered.shape[0]
     heads_here = w_qkv.shape[1] // (3 * HD)
-    projected = jnp.dot(
-        gathered,
-        lax.all_gather(w_qkv, "tile", axis=0, tiled=True),
-        preferred_element_type=jnp.float32,
-    )
+    projected = jnp.dot(gathered, ring_gather(w_qkv, "tile", 0), preferred_element_type=jnp.float32)
     full_out = lax.all_gather(w_out, "tile", axis=1, tiled=True)
     projected = projected.reshape(length, heads_here, 3, HD)
     queries = root_norm(projected[:, :, 0]).astype(jnp.bfloat16)

time: 438 us -> 372 us (0.85)
  waiting for transfers between devices: 323 us -> 226 us
  local copies, waits for them, and re-layouts: 9.9 us -> 38.6 us
    all_gather x1, waiting for transfers between devices: 112 us -> 0.01 us  [shards(): gathered = lax.all_gather(norm_in, 'seq', axis=0, tiled=True)]
    ppermute x0 -> x3, waiting for transfers between devices: none -> 107 us  [ring_gather(): lax.ppermute(pieces[far - 1], axis, [(d, (d - 1) % ways) for d in range(w...]
    all_gather x1 -> x0, waiting for transfers between devices: 92.7 us -> none  [shards(): lax.all_gather(w_qkv, 'tile', axis=0, tiled=True)]
    unnamed x25 -> x38, local copies, waits for them, and re-layouts: 7.19 us -> 31.7 us
    ppermute x0 -> x3, starting transfers between devices: none -> 4.57 us  [ring_gather(): lax.ppermute(pieces[far - 1], axis, [(d, (d - 1) % ways) for d in range(w...]
  transfers between devices with their start and end apart: 12 -> 14, of which waited for: 5 -> 7; matrix products, arithmetic and copies ran while one was open for 12% -> 21% of each run, Pallas kernels for 0% -> 0%
where the time goes in v1:
time: 372 us; the launch traced here: 369 us
  waiting for transfers between devices  226 us (61%)
  matrix products  50.2 us (13%)
  local copies, waits for them, and re-layouts  38.6 us (10%)
  starting transfers between devices  22.7 us (6%)
  other arithmetic  16.9 us (5%)
  between operations  14.9 us (4%)
    reduce_scatter x1, waiting for transfers between devices, shards(): lax.psum_scatter(jnp.dot(attended, full_out, preferred_element_type=jnp.f...  112 us
    ppermute x3, waiting for transfers between devices, ring_gather(): lax.ppermute(pieces[far - 1], axis, [(d, (d - 1) % ways) for d in range(w...  107 us
    unnamed x38, local copies, waits for them, and re-layouts  31.7 us
    dot_general x1, matrix products, shards(): jnp.dot(gathered, ring_gather(w_qkv, 'tile', 0), preferred_element_type=j...  19.7 us
    ppermute x8, starting transfers between devices, shifted(): lax.ppermute(value, axis, [(source, source + steps) for source in range(l...  18 us
    dot_general x2, matrix products, shards(): jnp.einsum('qhe,khe->hqk', queries[first:first + block], keys, preferred_...  10.9 us
    dot_general x1, matrix products, shards(): jnp.dot(attended, full_out, preferred_element_type=jnp.float32)  9.6 us
    dot_general x2, matrix products, shards(): jnp.einsum('hqk,khe->qhe', probs, values, preferred_element_type=jnp.floa...  8.92 us
  transfers between devices with their start and end apart: 14, of which 7 were waited for; matrix products, arithmetic and copies ran while one was open for 21% of the time, Pallas kernels for 0%

profile of v1, /device:TPU:26, one launch (start us, length us, event | category | flops | bytes accessed | tf_op | source)
XLA Modules:
  0.0 369.3 jit_solution(18213145232911290150)
XLA Ops:
  10.8 2.0 fusion.10
  12.8 1.9 fusion.13
  14.9 39.3 %collective-permute-done = bf16[768,2304]{1,0:T(8,128)(2,1)S(1)} collective-permute-done((bf16[768,2304]{1,0:T(8,128)(2,1)}, bf16[768,2304]{1,0:T(8,128)(2,1)S(1)}, u32[]{:S(2)}, u32[]{:S(2)}) %collective-permute-start) | collective-permute-done | bytes 3538976 | tf_op jit(solution)/shard_map/ppermute | solution.py:16
  55.9 2.2 collective-permute-start.1
  58.1 39.0 %collective-permute-done.1 = bf16[768,2304]{1,0:T(8,128)(2,1)} collective-permute-done((bf16[768,2304]{1,0:T(8,128)(2,1)S(1)}, bf16[768,2304]{1,0:T(8,128)(2,1)}, u32[]{:S(2)}, u32[]{:S(2)}) %collective-permute-start.1) | collective-permute-done | bytes 3538976 | tf_op jit(solution)/shard_map/ppermute | solution.py:16
  97.1 2.3 collective-permute-start.2
  99.6 4.1 %constant_dynamic-update-slice_fusion.7 = bf16[6144,2304]{1,0:T(8,128)(2,1)} fusion(bf16[768,2304]{1,0:T(8,128)(2,1)} %param.10), kind=kLoop, calls=%fused_computation.59 | loop fusion | bytes 7077888
  103.7 2.0 constant_dynamic-update-slice_fusion.6
  105.7 4.1 %constant_dynamic-update-slice_fusion.5 = bf16[6144,2304]{1,0:T(8,128)(2,1)} fusion(bf16[6144,2304]{1,0:T(8,128)(2,1)} %constant_dynamic-update-slice_fusion.6, bf16[768,2304]{1,0:T(8,128)(2,1)} %collective-permute-done.1), kind=kLoop, calls=%fused_computation.57 | loop fusion | bytes 7077888
  109.8 29.0 %collective-permute-done.2 = bf16[768,2304]{1,0:T(8,128)(2,1)} collective-permute-done((bf16[768,2304]{1,0:T(8,128)(2,1)}, bf16[768,2304]{1,0:T(8,128)(2,1)}, u32[]{:S(2)}, u32[]{:S(2)}) %collective-permute-start.2) | collective-permute-done | bytes 3538976 | tf_op jit(solution)/shard_map/ppermute | solution.py:16
  138.8 4.6 %constant_dynamic-update-slice_fusion.4 = bf16[6144,2304]{1,0:T(8,128)(2,1)} fusion(bf16[6144,2304]{1,0:T(8,128)(2,1)} %constant_dynamic-update-slice_fusion.5, bf16[768,2304]{1,0:T(8,128)(2,1)} %collective-permute-done.2), kind=kLoop, calls=%fused_computation.56 | loop fusion | bytes 7077888
  143.4 2.0 constant_dynamic-update-slice_fusion.3
  145.3 2.0 constant_dynamic-update-slice_fusion.2
  147.3 4.0 %constant_dynamic-update-slice_fusion.1 = bf16[6144,2304]{1,0:T(8,128)(2,1)} fusion(bf16[6144,2304]{1,0:T(8,128)(2,1)} %constant_dynamic-update-slice_fusion.2, bf16[768,2304]{1,0:T(8,128)(2,1)} %collective-permute-done.1), kind=kLoop, calls=%fused_computation.53 | loop fusion | bytes 7077888
  151.3 4.1 %constant_dynamic-update-slice_fusion = bf16[6144,2304]{1,0:T(8,128)(2,1)} fusion(bf16[6144,2304]{1,0:T(8,128)(2,1)} %constant_dynamic-update-slice_fusion.1, bf16[768,2304]{1,0:T(8,128)(2,1)} %collective-permute-done.2), kind=kLoop, calls=%fused_computation.52 | loop fusion | bytes 7077888 | tf_op jit(solution)/shard_map/jit(_roll_dynamic)/concatenate | solution.py:19
  155.5 19.7 %fusion = f32[1024,2304]{0,1:T(8,128)S(1)} fusion(bf16[1024,3072]{1,0:T(8,128)(2,1)} %all-gather.3.cloned.1.call-done, bf16[6144,2304]{1,0:T(8,128)(2,1)} %constant_dynamic-update-slice_fusion, s32[]{:T(128)S(6)} %select_n.42), kind=kOutput, calls=%fused_computation | convolution fusion | flops 14495514624 | bytes 29884420 | tf_op jit(solution)/shard_map/dot_general | solution.py:50
  175.2 3.5 copy-done.3
  178.7 2.1 slice.50
  180.8 3.6 copy.21
  184.4 2.9 fusion.14
  187.3 2.3 multiply_reduce_fusion.1
  190.7 8.2 %fusion.2 = (f32[6,512]{1,0:T(8,128)S(1)}, f32[6,512,1024]{2,1,0:T(8,128)}) fusion(f32[1024,6,3,128]{0,3,2,1:T(8,128)} %bitcast.77, f32[1024,6]{0,1:T(8,128)S(1)} %add_rsqrt_fusion, bf16[1024,6,128]{2,0,1:T(8,128)(2,1)S(1)} %fusion.15), kind=kOutput, calls=%fused_computation.6 | convolution fusion | flops 813167616 | bytes 16560128 | tf_op jit(solution)/shard_map/qhe,khe->hqk/dot_general | solution.py:61
  198.9 2.7 fusion.3
  201.6 6.0 %fusion.21 = bf16[512,6,128]{0,2,1:T(8,128)(2,1)S(1)} fusion(f32[6,512,1024]{2,1,0:T(8,128)} %get-tuple-element.14, f32[6,512]{1,0:T(8,128)S(1)} %get-tuple-element.13, f32[1024,6,3,128]{0,3,2,1:T(8,128)S(1)} %bitcast.81), kind=kOutput, calls=%fused_computation.37 | convolution fusion | flops 815136768 | bytes 14958592 | tf_op jit(solution)/shard_map/hqk,khe->qhe/dot_general | solution.py:72
  207.6 2.9 fusion.22
  210.7 9.6 %convolution_convert_fusion = bf16[1024,3072]{1,0:T(8,128)(2,1)} fusion(bf16[1024,768]{0,1:T(8,128)(2,1)S(1)} %bitcast.83, bf16[768,3072]{1,0:T(8,128)(2,1)} %all-gather.5.cloned.1.call-done), kind=kOutput, calls=%fused_computation.10 | convolution fusion | flops 4834983936 | bytes 12582912 | tf_op jit(solution)/shard_map/dot_general | solution.py:78
  221.1 111.7 %reduce-scatter.2.cloned.1.call-done = bf16[256,3072]{1,0:T(8,128)(2,1)} async-done(((bf16[1024,3072]{1,0:T(8,128)(2,1)}), bf16[256,3072]{1,0:T(8,128)(2,1)}) %reduce-scatter.2.cloned.1.call-update) | async-done | bytes 1572880 | tf_op jit(solution)/shard_map/reduce_scatter | solution.py:77
  332.9 2.1 fusion.16
  338.9 3.6 collective-permute-start.5
  344.5 2.4 collective-permute-start.7
  349.4 4.3 %collective-permute-start.8 = (bf16[256]{0:T(256)(128)(2,1)S(1)}, bf16[256]{0:T(256)(128)(2,1)S(1)}, u32[]{:S(2)}, u32[]{:S(2)}) collective-permute-start(bf16[256]{0:T(256)(128)(2,1)S(1)} %collective-permute-done.7), channel_id=1, source_target_pairs={{2,0},{3,1},{6,4},{7,5},{10,8},{11,9},{14,12},{15,13},{18,16},{19,... | collective-permute-start | bytes 1544 | tf_op jit(solution)/shard_map/ppermute | solution.py:25
  356.9 5.2 %collective-permute-done.6 = bf16[256,128]{0,1:T(8,128)(2,1)S(1)} collective-permute-done((bf16[256,128]{0,1:T(8,128)(2,1)S(1)}, bf16[256,128]{0,1:T(8,128)(2,1)S(1)}, u32[]{:S(2)}, u32[]{:S(2)}) %collective-permute-start.6) | collective-permute-done | bytes 65568 | tf_op jit(solution)/shard_map/ppermute | solution.py:25
  (69 shorter events, 18.9 us)
Async XLA Ops:
  7.2 328.7 %copy-start = (bf16[3072,64]{0,1:T(8,128)(2,1)S(1)}, bf16[3072,64]{0,1:T(8,128)(2,1)}, u32[]{:S(2)}) copy-start(bf16[3072,64]{0,1:T(8,128)(2,1)} %param.12) | copy-start | bytes 1179652
  7.2 5.6 %copy-start.1 = (bf16[1,256,3072]{2,1,0:T(8,128)(2,1)S(1)}, bf16[1,256,3072]{2,1,0:T(8,128)(2,1)}, u32[]{:S(2)}) copy-start(bf16[1,256,3072]{2,1,0:T(8,128)(2,1)} %param.8) | copy-start | bytes 4718596
  7.2 148.3 %all-gather.3.cloned.1.call-start = ((), (), s32[]{:S(2)}) async-start(), calls=%async_computation.1 | async-start | bytes 7864320 | tf_op jit(solution)/shard_map/all_gather | solution.py:47
  14.8 196.0 %all-gather.5.cloned.1.call-start = ((), (), s32[]{:S(2)}) async-start(), calls=%async_computation.2 | async-start | bytes 5898240 | tf_op jit(solution)/shard_map/all_gather | solution.py:51
  14.8 39.4 %collective-permute-start = (bf16[768,2304]{1,0:T(8,128)(2,1)}, bf16[768,2304]{1,0:T(8,128)(2,1)S(1)}, u32[]{:S(2)}, u32[]{:S(2)}) collective-permute-start(bf16[768,2304]{1,0:T(8,128)(2,1)} %param.10), channel_id=1, source_target_pairs={{0,12},{4,0},{8,4},{12,8},{1,13},{5,1},{9,5},{13,9},{2,14},{6,2},{... | collective-permute-start | bytes 10616840 | tf_op jit(solution)/shard_map/ppermute | solution.py:16
  54.2 1.7 copy-start.5
  55.9 41.2 %collective-permute-start.1 = (bf16[768,2304]{1,0:T(8,128)(2,1)S(1)}, bf16[768,2304]{1,0:T(8,128)(2,1)}, u32[]{:S(2)}, u32[]{:S(2)}) collective-permute-start(bf16[768,2304]{1,0:T(8,128)(2,1)S(1)} %collective-permute-done), channel_id=1, source_target_pairs={{0,12},{4,0},{8,4},{12,8},{1,13},{5,1},{9,5},{13,9},{2,14},{6,2},{... | collective-permute-start | bytes 10616840 | tf_op jit(solution)/shard_map/ppermute | solution.py:16
  97.1 41.6 %collective-permute-start.2 = (bf16[768,2304]{1,0:T(8,128)(2,1)}, bf16[768,2304]{1,0:T(8,128)(2,1)}, u32[]{:S(2)}, u32[]{:S(2)}) collective-permute-start(bf16[768,2304]{1,0:T(8,128)(2,1)} %collective-permute-done.1), channel_id=1, source_target_pairs={{0,12},{4,0},{8,4},{12,8},{1,13},{5,1},{9,5},{13,9},{2,14},{6,2},{... | collective-permute-start | bytes 10616840 | tf_op jit(solution)/shard_map/ppermute | solution.py:16
  99.5 233.4 %reduce-scatter.2.cloned.1.call-start = ((), (), s32[]{:S(2)}) async-start(), calls=%async_computation.3 | async-start | bytes 7864320 | tf_op jit(solution)/shard_map/reduce_scatter | solution.py:77
  99.6 4.1 %copy-start.6 = (bf16[768,2304]{1,0:T(8,128)(2,1)S(1)}, bf16[768,2304]{1,0:T(8,128)(2,1)}, u32[]{:S(2)}) copy-start(bf16[768,2304]{1,0:T(8,128)(2,1)} %copy-done.5) | copy-start | bytes 10616836
  109.8 33.6 %copy-start.4 = (bf16[768,2304]{1,0:T(8,128)(2,1)S(1)}, bf16[768,2304]{1,0:T(8,128)(2,1)}, u32[]{:S(2)}) copy-start(bf16[768,2304]{1,0:T(8,128)(2,1)} %param.10) | copy-start | bytes 10616836
  175.2 3.6 copy-start.3
  184.4 5.3 %copy-start.2 = (f32[1024,6,1,128]{3,0,1,2:T(8,128)S(1)}, f32[1024,6,1,128]{3,0,1,2:T(8,128)}, u32[]{:S(2)}) copy-start(f32[1024,6,1,128]{3,0,1,2:T(8,128)} %copy.21) | copy-start | bytes 9437188
  189.7 9.2 %slice-start = ((s8[9437184]{0:T(1024)(128)(4,1)}), s8[4194304]{0:T(1024)(128)(4,1)S(1)}, s32[]{:S(2)}) async-start(s8[9437184]{0:T(1024)(128)(4,1)} %bitcast.78), calls=%async_computation.4 | async-start | bytes 8388608
  190.6 8.2 %slice-start.1 = ((s8[9437184]{0:T(1024)(128)(4,1)}), s8[4194304]{0:T(1024)(128)(4,1)S(1)}, s32[]{:S(2)}) async-start(s8[9437184]{0:T(1024)(128)(4,1)} %bitcast.78), calls=%async_computation.5 | async-start | bytes 8388608
  190.7 8.2 %slice-start.2 = ((s8[9437184]{0:T(1024)(128)(4,1)}), s8[1048576]{0:T(1024)(128)(4,1)S(1)}, s32[]{:S(2)}) async-start(s8[9437184]{0:T(1024)(128)(4,1)} %bitcast.78), calls=%async_computation.6 | async-start | bytes 2097152
  220.3 0.7 copy-start.10
  332.9 2.1 copy-start.7
  332.9 3.0 copy-start.8
  332.9 3.0 copy-start.9
  332.9 3.0 copy-start.11
  337.0 16.7 %collective-permute-start.3 = (bf16[256,128]{0,1:T(8,128)(2,1)S(1)}, bf16[256,128]{0,1:T(8,128)(2,1)S(1)}, u32[]{:S(2)}, u32[]{:S(2)}) collective-permute-start(bf16[256,128]{0,1:T(8,128)(2,1)S(1)} %fusion.29), channel_id=1, source_target_pairs={{0,4},{4,8},{8,12},{1,5},{5,9},{9,13},{2,6},{6,10},{10,14},{3,7},{... | collective-permute-start | bytes 196616 | tf_op jit(solution)/shard_map/ppermute | solution.py:25
  338.9 16.1 %collective-permute-start.5 = (bf16[256,128]{0,1:T(8,128)(2,1)S(1)}, bf16[256,128]{0,1:T(8,128)(2,1)S(1)}, u32[]{:S(2)}, u32[]{:S(2)}) collective-permute-start(bf16[256,128]{0,1:T(8,128)(2,1)S(1)} %fusion.29), channel_id=1, source_target_pairs={{4,0},{8,4},{12,8},{5,1},{9,5},{13,9},{6,2},{10,6},{14,10},{7,3},{... | collective-permute-start | bytes 196616 | tf_op jit(solution)/shard_map/ppermute | solution.py:25
  342.6 4.3 %collective-permute-start.9 = (bf16[256]{0:T(256)(128)(2,1)S(1)}, bf16[256]{0:T(256)(128)(2,1)S(1)}, u32[]{:S(2)}, u32[]{:S(2)}) collective-permute-start(bf16[256]{0:T(256)(128)(2,1)S(1)} %convert_element_type.109), channel_id=1, source_target_pairs={{4,0},{8,4},{12,8},{5,1},{9,5},{13,9},{6,2},{10,6},{14,10},{7,3},{... | collective-permute-start | bytes 1544 | tf_op jit(solution)/shard_map/ppermute | solution.py:25
  344.5 4.9 %collective-permute-start.7 = (bf16[256]{0:T(256)(128)(2,1)S(1)}, bf16[256]{0:T(256)(128)(2,1)S(1)}, u32[]{:S(2)}, u32[]{:S(2)}) collective-permute-start(bf16[256]{0:T(256)(128)(2,1)S(1)} %convert_element_type.109), channel_id=1, source_target_pairs={{0,4},{4,8},{8,12},{1,5},{5,9},{9,13},{2,6},{6,10},{10,14},{3,7},{... | collective-permute-start | bytes 1544 | tf_op jit(solution)/shard_map/ppermute | solution.py:25
  346.9 9.4 %collective-permute-start.10 = (bf16[256]{0:T(256)(128)(2,1)S(1)}, bf16[256]{0:T(256)(128)(2,1)S(1)}, u32[]{:S(2)}, u32[]{:S(2)}) collective-permute-start(bf16[256]{0:T(256)(128)(2,1)S(1)} %collective-permute-done.9), channel_id=1, source_target_pairs={{0,2},{1,3},{4,6},{5,7},{8,10},{9,11},{12,14},{13,15},{16,18},{17,... | collective-permute-start | bytes 1544 | tf_op jit(solution)/shard_map/ppermute | solution.py:25
  349.4 6.9 %collective-permute-start.8 = (bf16[256]{0:T(256)(128)(2,1)S(1)}, bf16[256]{0:T(256)(128)(2,1)S(1)}, u32[]{:S(2)}, u32[]{:S(2)}) collective-permute-start(bf16[256]{0:T(256)(128)(2,1)S(1)} %collective-permute-done.7), channel_id=1, source_target_pairs={{2,0},{3,1},{6,4},{7,5},{10,8},{11,9},{14,12},{15,13},{18,16},{19,... | collective-permute-start | bytes 1544 | tf_op jit(solution)/shard_map/ppermute | solution.py:25
  353.7 3.2 collective-permute-start.4
  355.0 7.1 %collective-permute-start.6 = (bf16[256,128]{0,1:T(8,128)(2,1)S(1)}, bf16[256,128]{0,1:T(8,128)(2,1)S(1)}, u32[]{:S(2)}, u32[]{:S(2)}) collective-permute-start(bf16[256,128]{0,1:T(8,128)(2,1)S(1)} %collective-permute-done.5), channel_id=1, source_target_pairs={{0,2},{1,3},{4,6},{5,7},{8,10},{9,11},{12,14},{13,15},{16,18},{17,... | collective-permute-start | bytes 196616 | tf_op jit(solution)/shard_map/ppermute | solution.py:25
Sparse Core Ops, SparseCore 0:
  14.9 113.4 all-gather.2
  129.9 37.5 all-gather.4
  220.5 112.3 reduce-scatter.1
